TPU v7x, 32 devices: a whole 2x2x4 slice. The times are simulated.
32 devices in a mesh: brick: 8 (over y, x, core), help: 4 (over z).
Axes of the slice: x: 2, y: 2, z: 4, core: 2. Of those that a mesh axis runs over, the one named last changes fastest.
Arguments:
- positions: float32 [3, 2048], P(None, ('brick', 'help')), may hold values from 0 to 1
- velocities: float32 [3, 2048], P(None, ('brick', 'help')), may hold values from -5 to 5
- forces_in: float32 [3, 2048], P(None, ('brick', 'help')), may hold values from -5 to 5
- neighbors: int32 [2048, 128], P(('brick', 'help')), may hold values from -1 to 767, as said below
- w_embed1: float32 [32], replicated, may hold values from -4 to 4
- b_embed1: float32 [32], replicated, may hold values from -3 to 3
- w_embed2: bfloat16 [32, 64], replicated, may hold values from -1 to 1
- b_embed2: float32 [64], replicated, may hold values from -3 to 3
- w_embed3: bfloat16 [64, 128], replicated, may hold values from -0.75 to 0.75
- b_embed3: float32 [128], replicated, may hold values from -3 to 3
- w_fit1: bfloat16 [2048, 240], replicated, may hold values from -0.125 to 0.125
- b_fit1: float32 [240], replicated, may hold values from -3 to 3
- w_fit2: bfloat16 [240, 240], replicated, may hold values from -0.375 to 0.375
- b_fit2: float32 [240], replicated, may hold values from -3 to 3
- w_out: float32 [240], replicated, may hold values from -0.375 to 0.375
Outputs:
- positions_out: float32 [3, 2048], P(None, ('brick', 'help'))
- velocities_out: float32 [3, 2048], P(None, ('brick', 'help'))
- energy: float32 [2048], P(('brick', 'help'))
- forces_out: float32 [3, 2048], P(None, ('brick', 'help'))
Inputs may be any that keep to these rules, and one draw needn't show every extreme that they name: `neighbors`: row i holds atom i's neighbours as table entries: 0 to 255 the atoms of the brick before its own (cyclically), 256 to 511 its own brick, 512 to 767 the brick after; -1 pads. Live entries come first, an entry may repeat, an atom never lists itself. In the first half of the bricks an atom has 96 to 128 live entries, in the other bricks 128 / 4 to 64.
All inputs are finite; a program needn't handle non-finite values.
Results may differ from a plain program's by a relative error of at most 0.011.
Values sent between devices are 32-bit elements; how exact they have to be, the bound alone decides.
No kernel may reach another device: no remote copies, remote signals or barrier semaphores. Data moves between devices by JAX's collectives and lax.ppermute only.
A program may use at most 64 MiB of HBM per device.

v0:
```python
import jax
import jax.numpy as jnp
from jax import lax
from jax.sharding import PartitionSpec as P

NEIGHBOUR_SLOTS = 128
M2 = 16
STEPS = 2
kick_scale = 0.25
time_step = 0.05
highest_precision = lax.Precision.HIGHEST


def extended(value, sides, width):
    for axis, dim in sides:
        size, length = (lax.axis_size(axis), value.shape[dim])
        up = [(i, (i + 1) % size) for i in range(size)]
        down = [(j, i) for i, j in up]
        last = lax.slice_in_dim(value, length - width, length, axis=dim)
        first = lax.slice_in_dim(value, 0, width, axis=dim)
        before = lax.ppermute(last, axis, up)
        after = lax.ppermute(first, axis, down)
        value = jnp.concatenate([before, value, after], axis=dim)
    return value


def pair_terms(displace, live_mask, weights):
    (
        w_embed1,
        b_embed1,
        w_embed2,
        b_embed2,
        w_embed3,
        b_embed3,
        w_fit1,
        b_fit1,
        w_fit2,
        b_fit2,
        w_out,
    ) = weights
    blocks, slot_count = live_mask.shape
    quad_dist = jnp.sum(displace * displace, axis=0) + 0.25
    radius = jnp.sqrt(quad_dist)
    smooth = live_mask / radius
    environment_matrix = jnp.concatenate(
        [smooth[None], live_mask[None] * displace / quad_dist[None]], axis=0
    ).astype(jnp.bfloat16)
    flat_smooth = smooth.reshape(1, -1)
    hidden_first = jnp.tanh(w_embed1[:, None] * flat_smooth + b_embed1[:, None])
    pre_second = (
        jnp.dot(w_embed2.T, hidden_first.astype(jnp.bfloat16), preferred_element_type=jnp.float32)
        + b_embed2[:, None]
    )
    tanh_second = jnp.tanh(pre_second)
    hidden_second = jnp.concatenate([hidden_first, hidden_first], axis=0) + tanh_second
    pre_third = (
        jnp.dot(w_embed3.T, hidden_second.astype(jnp.bfloat16), preferred_element_type=jnp.float32)
        + b_embed3[:, None]
    )
    tanh_third = jnp.tanh(pre_third)
    embedding = (jnp.concatenate([hidden_second, hidden_second], axis=0) + tanh_third).astype(
        jnp.bfloat16
    )
    embedding_width = embedding.shape[0]
    embedding_rows = embedding.reshape(embedding_width, blocks, slot_count)
    descriptor_tensor = (
        jnp.einsum(
            "srj,lrj->rsl", environment_matrix, embedding_rows, preferred_element_type=jnp.float32
        )
        / NEIGHBOUR_SLOTS
    )
    axis_part = descriptor_tensor[:, :, :M2]
    descriptor = jnp.einsum(
        "bce,bck->bek", descriptor_tensor, axis_part, precision=highest_precision
    )
    flat_descr = descriptor.reshape(blocks, -1).astype(jnp.bfloat16)
    fit_hidden = jnp.tanh(jnp.dot(flat_descr, w_fit1, preferred_element_type=jnp.float32) + b_fit1)
    pre_out = (
        jnp.dot(fit_hidden.astype(jnp.bfloat16), w_fit2, preferred_element_type=jnp.float32)
        + b_fit2
    )
    tanh_out = jnp.tanh(pre_out)
    energy = jnp.dot(fit_hidden + tanh_out, w_out, precision=highest_precision)
    grad_out = (w_out[None, :] * (1.0 - tanh_out * tanh_out)).astype(jnp.bfloat16)
    grad_fit = w_out[None, :] + jnp.dot(grad_out, w_fit2.T, preferred_element_type=jnp.float32)
    grad_act = (grad_fit * (1.0 - fit_hidden * fit_hidden)).astype(jnp.bfloat16)
    grad_descr = jnp.dot(grad_act, w_fit1.T, preferred_element_type=jnp.float32).reshape(
        blocks, embedding_width, -1
    )
    grad_tensor = jnp.einsum("bek,bck->bce", grad_descr, axis_part, precision=highest_precision)
    extra_grad = jnp.einsum(
        "bek,bce->bck", grad_descr, descriptor_tensor, precision=highest_precision
    )
    grad_tensor = grad_tensor + jnp.pad(
        extra_grad, ((0, 0), (0, 0), (0, embedding_width - extra_grad.shape[2]))
    )
    descriptor_product_gradient = grad_tensor.astype(jnp.bfloat16)
    environment_gradient = (
        jnp.einsum(
            "ohm,hdo->dhm",
            embedding_rows,
            descriptor_product_gradient,
            preferred_element_type=jnp.float32,
        )
        / NEIGHBOUR_SLOTS
    )
    embedding_gradient = (
        jnp.einsum(
            "zmj,mzr->rmj",
            environment_matrix,
            descriptor_product_gradient,
            preferred_element_type=jnp.float32,
        ).reshape(embedding_width, -1)
        / NEIGHBOUR_SLOTS
    )
    grad_third = (embedding_gradient * (1.0 - tanh_third * tanh_third)).astype(jnp.bfloat16)
    half_width = embedding_width // 2
    grad_hidden2 = (
        embedding_gradient[:half_width]
        + embedding_gradient[half_width:]
        + jnp.dot(w_embed3, grad_third, preferred_element_type=jnp.float32)
    )
    grad_second = (grad_hidden2 * (1.0 - tanh_second * tanh_second)).astype(jnp.bfloat16)
    quarter = half_width // 2
    grad_hidden1 = (
        grad_hidden2[:quarter]
        + grad_hidden2[quarter:]
        + jnp.dot(w_embed2, grad_second, preferred_element_type=jnp.float32)
    )
    grad_smooth = (
        jnp.dot(
            w_embed1,
            grad_hidden1 * (1.0 - hidden_first * hidden_first),
            precision=highest_precision,
        ).reshape(blocks, slot_count)
        + environment_gradient[0]
    )
    radial = jnp.sum(environment_gradient[1:] * displace, axis=0)
    factor = -grad_smooth / (radius * quad_dist) - 2.0 * radial / (quad_dist * quad_dist)
    pair_grad = live_mask[None] * (
        displace * factor[None] + environment_gradient[1:] / quad_dist[None]
    )
    return (energy, pair_grad)


def ghost_table(coords):
    stacked = coords[:, None, :]
    brick_pos = lax.all_gather(stacked, "help", axis=2, tiled=True)
    gathered = extended(brick_pos, (("brick", 1),), 1)
    return gathered.reshape(3, -1)


def return_forces(gathered):
    reduced = lax.psum_scatter(gathered, "help", scatter_dimension=2, tiled=True)
    padded = extended(reduced, (("brick", 1),), 1)
    returned = padded[:, 0] + padded[:, 2] + padded[:, 4]
    return returned


def evaluate(coords, neighbors, weights):
    ghost = ghost_table(coords)
    brick_len = ghost.shape[1] // 3
    atom_count = coords.shape[1]
    safe_index = jnp.maximum(neighbors, 0)
    live_mask = (neighbors >= 0).astype(jnp.float32)
    shift_x = (safe_index // brick_len - 1).astype(jnp.float32)
    block_size = 32
    block_count = atom_count // block_size

    def one_block(pieces):
        own_pos, table_index, offset, mask_rows = pieces
        neighbour_pos = jnp.take(ghost, table_index, axis=1)
        displace = neighbour_pos - own_pos[:, :, None]
        displace = (
            jnp.concatenate([displace[:1] + offset[None], displace[1:]], axis=0) * mask_rows[None]
        )
        return pair_terms(displace, mask_rows, weights)

    own_blocks = coords.reshape(3, block_count, block_size).transpose(1, 0, 2)
    energy, pair_grads = lax.map(
        one_block,
        (
            own_blocks,
            safe_index.reshape(block_count, block_size, -1),
            shift_x.reshape(block_count, block_size, -1),
            live_mask.reshape(block_count, block_size, -1),
        ),
    )
    pair_grads = pair_grads.transpose(1, 0, 2, 3).reshape(3, atom_count, -1)
    energy_rows = energy.reshape(-1)
    gathered = jnp.zeros((3, 3 * brick_len), jnp.float32).at[:, safe_index].add(pair_grads)
    returned = return_forces(gathered.reshape(3, 3, brick_len))
    return (energy_rows, jnp.sum(pair_grads, axis=2) - returned)


def local(
    positions,
    velocities,
    forces_in,
    neighbors,
    w_embed1,
    b_embed1,
    w_embed2,
    b_embed2,
    w_embed3,
    b_embed3,
    w_fit1,
    b_fit1,
    w_fit2,
    b_fit2,
    w_out,
):
    weights = (
        w_embed1,
        b_embed1,
        w_embed2,
        b_embed2,
        w_embed3,
        b_embed3,
        w_fit1,
        b_fit1,
        w_fit2,
        b_fit2,
        w_out,
    )
    coords = positions
    speed = velocities
    force_now = forces_in
    energy = jnp.zeros((positions.shape[1],), jnp.float32)
    for md_step in range(STEPS):
        speed = speed + kick_scale * force_now
        coords = coords + time_step * speed
        energy, force_now = evaluate(coords, neighbors, weights)
        speed = speed + kick_scale * force_now
    return (coords, speed, energy, force_now)


def solution(mesh):
    return jax.shard_map(
        local,
        mesh=mesh,
        in_specs=(
            P(None, ("brick", "help")),
            P(None, ("brick", "help")),
            P(None, ("brick", "help")),
            P(("brick", "help"), None),
            P(),
            P(),
            P(),
            P(),
            P(),
            P(),
            P(),
            P(),
            P(),
            P(),
            P(),
        ),
        out_specs=(
            P(None, ("brick", "help")),
            P(None, ("brick", "help")),
            P(("brick", "help")),
            P(None, ("brick", "help")),
        ),
        check_vma=False,
    )
```

profile of v0, /device:TPU:0, one launch (start us, length us, event | category | flops | bytes accessed | tf_op | source)
XLA Modules:
  0.0 359.1 jit_solution(11644134132301394717)
XLA Ops:
  7.9 13.6 %all-gather.2 = f32[4,64,3]{1,2,0:T(4,128)S(1)} all-gather(f32[1,64,3]{1,2,0:T(4,128)S(1)} %bitcast.479), channel_id=2, replica_groups=mesh['brick'=8,'help'=4] {'help'}, dimensions={0}, use_global_device_ids=true | all-gather | bytes 3840 | tf_op jit(solution)/shard_map/all_gather | solution.py:148
  22.9 1.4 fusion.116
  24.5 1.1 collective-permute-done
  26.5 71.5 %while.26 = (s32[]{:T(128)}, f32[2,3,32,128]{3,1,2,0:T(4,128)}, f32[2,32,128]{2,0,1:T(2,128)S(1)}, s32[2,32,128]{2,1,0:T(8,128)}, f32[3,768]{0,1:T(8,128)S(1)}, ...) while((s32[]{:T(128)}, f32[2,3,32,128]{3,1,2,0:T(4,128)}, ...), condition=%wide.region_3.5_spmd, body=%wide.region_0.4_spmd.sunk | while | flops 271267840 | bytes 53851500 | solution.py:180
  27.4 10.8 %gather_fusion = f32[4096,3]{1,0:T(8,128)S(1)} fusion(f32[3,768]{0,1:T(8,128)S(1)} %get-tuple-element.963, s32[4096]{0:T(1024)S(1)} %bitcast_clamp_fusion.4), kind=kCustom, calls=%fused_computation.clone.clone.1 | custom fusion | bytes 114688 | tf_op jit(solution)/shard_map/while/body/eval_jaxpr/jit(_take)/gather | solution.py:172
  40.7 2.1 maximum_add_fusion.6
  42.9 1.2 fusion.262
  47.2 1.2 copy.233
  48.5 1.4 fusion.265
  51.0 1.5 fusion.267
  52.5 1.8 copy.234
  54.3 1.4 fusion.268
  55.6 1.2 fusion.269
  57.8 1.4 fusion.271
  59.2 1.0 fusion.272
  60.4 1.1 fusion.273
  63.1 10.8 %gather_fusion = f32[4096,3]{1,0:T(8,128)S(1)} fusion(f32[3,768]{0,1:T(8,128)S(1)} %get-tuple-element.963, s32[4096]{0:T(1024)S(1)} %bitcast_clamp_fusion.4), kind=kCustom, calls=%fused_computation.clone.clone.1 | custom fusion | bytes 114688 | tf_op jit(solution)/shard_map/while/body/eval_jaxpr/jit(_take)/gather | solution.py:172
  76.5 2.1 maximum_add_fusion.6
  78.6 1.2 fusion.262
  83.0 1.2 copy.233
  84.2 1.4 fusion.265
  86.7 1.5 fusion.267
  88.3 1.8 copy.234
  90.0 1.4 fusion.268
  91.4 1.2 fusion.269
  93.5 1.4 fusion.271
  95.0 1.0 fusion.272
  96.1 1.1 fusion.273
  98.0 3.5 copy.144
  101.6 45.3 %scatter_custom_fusion = f32[3,768]{0,1:T(8,128)S(1)} fusion(s32[8192]{0:T(1024)} %get-tuple-element.670, f32[8192,3]{1,0:T(8,128)} %bitcast.458, f32[]{:T(128)} %constant.160.clone.1), kind=kCustom, calls=%fused_computation.189 | custom fusion | flops 24576 | bytes 9728 | tf_op jit(solution)/shard_map/scatter-add | solution.py:191
  148.1 24.3 %reduce-scatter.7.cloned.1.call-done = f32[64,9]{1,0:T(8,128)} async-done(((f32[256,9]{1,0:T(8,128)}), f32[64,9]{1,0:T(8,128)}) %reduce-scatter.7.cloned.1.call-update) | async-done | bytes 2320
  174.7 2.7 collective-permute-done.2
  178.0 11.9 %all-gather.3 = f32[4,64,3]{1,2,0:T(4,128)S(1)} all-gather(f32[1,64,3]{1,2,0:T(4,128)S(1)} %bitcast.480), channel_id=3, replica_groups=mesh['brick'=8,'help'=4] {'help'}, dimensions={0}, use_global_device_ids=true | all-gather | bytes 3840 | tf_op jit(solution)/shard_map/all_gather | solution.py:148
  191.4 2.8 collective-permute-done.4
  195.8 77.6 %while.27 = (s32[]{:T(128)}, f32[2,32]{1,0:T(2,128)}, f32[2,3,32,128]{3,1,2,0:T(4,128)}, f32[2,32,128]{2,0,1:T(2,128)S(1)}, s32[2,32,128]{2,1,0:T(8,128)}, /*ind...) while((s32[]{:T(128)}, f32[2,32]{1,0:T(2,128)}, ...), condition=%wide.region_10.12_spmd, body=%wide.region_7.11_spmd.sunk | while | flops 271367680 | bytes 45020100 | solution.py:180
  196.6 11.8 %gather_fusion.1 = f32[4096,3]{1,0:T(8,128)S(1)} fusion(f32[3,768]{0,1:T(8,128)} %get-tuple-element.1025, s32[4096]{0:T(1024)S(1)} %bitcast_clamp_fusion.5), kind=kCustom, calls=%fused_computation.1.clone.clone.1 | custom fusion | bytes 114688 | tf_op jit(solution)/shard_map/while/body/eval_jaxpr/jit(_take)/gather | solution.py:172
  211.0 2.1 maximum_add_fusion.7
  213.1 1.2 fusion.301
  217.4 1.2 copy.241
  218.7 1.4 fusion.304
  221.1 1.3 dynamic_update_slice.27
  222.4 2.4 fusion.307
  224.7 1.7 copy.242
  227.3 1.6 fusion.310
  228.9 1.3 multiply_bitcast_fusion.7
  230.2 1.4 fusion.311
  232.8 1.1 fusion.313
  235.4 11.8 %gather_fusion.1 = f32[4096,3]{1,0:T(8,128)S(1)} fusion(f32[3,768]{0,1:T(8,128)} %get-tuple-element.1025, s32[4096]{0:T(1024)S(1)} %bitcast_clamp_fusion.5), kind=kCustom, calls=%fused_computation.1.clone.clone.1 | custom fusion | bytes 114688 | tf_op jit(solution)/shard_map/while/body/eval_jaxpr/jit(_take)/gather | solution.py:172
  249.7 2.1 maximum_add_fusion.7
  251.8 1.2 fusion.301
  256.2 1.2 copy.241
  257.4 1.4 fusion.304
  259.9 1.3 dynamic_update_slice.27
  261.1 2.4 fusion.307
  263.5 1.7 copy.242
  266.1 1.6 fusion.310
  267.7 1.3 multiply_bitcast_fusion.7
  269.0 1.4 fusion.311
  271.6 1.1 fusion.313
  273.4 3.5 copy.152
  276.9 45.2 %scatter_custom_fusion.1 = f32[3,768]{0,1:T(8,128)S(1)} fusion(s32[8192]{0:T(1024)} %get-tuple-element.670, f32[8192,3]{1,0:T(8,128)} %bitcast.457, f32[]{:T(128)} %constant.160.clone.1), kind=kCustom, calls=%fused_computation.187 | custom fusion | flops 24576 | bytes 9728 | tf_op jit(solution)/shard_map/scatter-add | solution.py:191
  323.3 23.3 %reduce-scatter.9.cloned.1.call-done = f32[64,9]{1,0:T(8,128)} async-done(((f32[256,9]{1,0:T(8,128)}), f32[64,9]{1,0:T(8,128)}) %reduce-scatter.9.cloned.1.call-update) | async-done | bytes 2320
  348.5 1.3 reshape.307
  349.8 1.8 collective-permute-done.6
  (385 shorter events, 52.5 us)
Async XLA Ops:
  7.2 165.2 %reduce-scatter.7.cloned.1.call-start = ((), (), s32[]{:S(2)}) async-start(), calls=%async_computation.2 | async-start | bytes 163840
  7.9 18.6 %copy-start.58 = (f32[3,64]{1,0:T(4,128)}, f32[3,64]{1,0:T(4,128)S(1)}, u32[]{:S(2)}) copy-start(f32[3,64]{1,0:T(4,128)S(1)} %multiply_add_fusion.2) | copy-start | bytes 2308
  21.6 2.8 collective-permute-start.1
  21.7 4.0 %collective-permute-start = (f32[3,1,256]{2,0,1:T(4,128)S(1)}, f32[3,1,256]{2,0,1:T(4,128)S(1)}, u32[]{:S(2)}, u32[]{:S(2)}) collective-permute-start(f32[3,1,256]{2,0,1:T(4,128)S(1)} %bitcast.482), channel_id=1, source_target_pairs={{0,4},{4,8},{8,12},{12,16},{16,20},{20,24},{24,28},{28,0},{1,5},{5... | collective-permute-start | bytes 9224 | tf_op jit(solution)/shard_map/ppermute | solution.py:21
  26.5 16.3 %copy-start.14 = (f32[3,768]{0,1:T(8,128)}, f32[3,768]{0,1:T(8,128)S(1)}, u32[]{:S(2)}) copy-start(f32[3,768]{0,1:T(8,128)S(1)} %get-tuple-element.963) | copy-start | bytes 27652 | tf_op jit(solution)/shard_map/while
  26.5 16.3 %copy-start.36 = (f32[2,32,128]{2,0,1:T(2,128)}, f32[2,32,128]{2,0,1:T(2,128)S(1)}, u32[]{:S(2)}) copy-start(f32[2,32,128]{2,0,1:T(2,128)S(1)} %get-tuple-element.961) | copy-start | bytes 98308 | tf_op jit(solution)/shard_map/while
  26.5 16.3 %copy-start.40 = (f32[2,32,128]{2,0,1:T(2,128)}, f32[2,32,128]{2,0,1:T(2,128)S(1)}, u32[]{:S(2)}) copy-start(f32[2,32,128]{2,0,1:T(2,128)S(1)} %get-tuple-element.965) | copy-start | bytes 98308 | tf_op jit(solution)/shard_map/while
  26.5 16.3 %copy-start.56 = (f32[2,3,32]{2,1,0:T(4,128)}, f32[2,3,32]{2,1,0:T(4,128)S(1)}, u32[]{:S(2)}) copy-start(f32[2,3,32]{2,1,0:T(4,128)S(1)} %get-tuple-element.964) | copy-start | bytes 2308 | tf_op jit(solution)/shard_map/while
  26.5 14.2 %copy-start.34 = (bf16[32,64]{1,0:T(8,128)(2,1)S(1)}, bf16[32,64]{1,0:T(8,128)(2,1)}, u32[]{:S(2)}) copy-start(bf16[32,64]{1,0:T(8,128)(2,1)} %get-tuple-element.968) | copy-start | bytes 12292 | tf_op jit(solution)/shard_map/while
  39.7 4.6 %copy-start.18 = (f32[1,32,128]{2,0,1:T(1,128)}, f32[1,32,128]{2,0,1:T(1,128)S(1)}, u32[]{:S(2)}) copy-start(f32[1,32,128]{2,0,1:T(1,128)S(1)} %get-tuple-element.891) | copy-start | bytes 49156 | tf_op jit(solution)/shard_map/while
  39.8 4.6 %copy-start.12 = (f32[2,32,128]{2,0,1:T(2,128)}, f32[2,32,128]{2,0,1:T(2,128)S(1)}, u32[]{:S(2)}) copy-start(f32[2,32,128]{2,0,1:T(2,128)S(1)} %slice.243) | copy-start | bytes 98308 | tf_op jit(solution)/shard_map/while
  39.9 4.2 %copy-start.25 = (f32[4096]{0:T(1024)}, f32[4096]{0:T(1024)S(1)}, u32[]{:S(2)}) copy-start(f32[4096]{0:T(1024)S(1)} %bitcast_multiply_fusion.6) | copy-start | bytes 49156 | tf_op jit(solution)/shard_map/while
  44.3 4.1 %copy-start = (bf16[2048,240]{0,1:T(8,128)(2,1)S(1)}, bf16[2048,240]{0,1:T(8,128)(2,1)}, u32[]{:S(2)}) copy-start(bf16[2048,240]{0,1:T(8,128)(2,1)} %get-tuple-element.973) | copy-start | bytes 2949124 | tf_op jit(solution)/shard_map/while
  44.3 5.6 %copy-start.7 = (bf16[240,240]{1,0:T(8,128)(2,1)S(1)}, bf16[240,240]{1,0:T(8,128)(2,1)}, u32[]{:S(2)}) copy-start(bf16[240,240]{1,0:T(8,128)(2,1)} %get-tuple-element.975) | copy-start | bytes 345604 | tf_op jit(solution)/shard_map/while
  44.3 5.6 %copy-start.50 = (f32[240]{0:T(256)S(1)}, f32[240]{0:T(256)}, u32[]{:S(2)}) copy-start(f32[240]{0:T(256)} %get-tuple-element.976) | copy-start | bytes 2884 | tf_op jit(solution)/shard_map/while
  46.5 4.4 %copy-start.9 = (f32[32,4,128]{2,1,0:T(4,128)}, f32[32,4,128]{2,1,0:T(4,128)S(1)}, u32[]{:S(2)}) copy-start(f32[32,4,128]{2,1,0:T(4,128)S(1)} %convolution_multiply_fusion.6) | copy-start | bytes 196612 | tf_op jit(solution)/shard_map/while
  52.5 4.3 %copy-start.4 = (bf16[16,32,8,128]{3,2,1,0:T(8,128)(2,1)S(1)}, bf16[16,32,8,128]{3,2,1,0:T(8,128)(2,1)}, u32[]{:S(2)}) copy-start(bf16[16,32,8,128]{3,2,1,0:T(8,128)(2,1)} %copy-done.3) | copy-start | bytes 3145732 | tf_op jit(solution)/shard_map/while
  52.5 4.7 %copy-start.22 = (bf16[3,32,128]{2,0,1:T(4,128)(2,1)S(1)}, bf16[3,32,128]{2,0,1:T(4,128)(2,1)}, u32[]{:S(2)}) copy-start(bf16[3,32,128]{2,0,1:T(4,128)(2,1)} %copy-done.21) | copy-start | bytes 73732 | tf_op jit(solution)/shard_map/while
  52.5 4.7 %copy-start.33 = (bf16[1,32,128]{2,0,1:T(2,128)(2,1)S(1)}, bf16[1,32,128]{2,0,1:T(2,128)(2,1)}, u32[]{:S(2)}) copy-start(bf16[1,32,128]{2,0,1:T(2,128)(2,1)} %copy-done.32) | copy-start | bytes 24580 | tf_op jit(solution)/shard_map/while
  62.3 16.3 %copy-start.14 = (f32[3,768]{0,1:T(8,128)}, f32[3,768]{0,1:T(8,128)S(1)}, u32[]{:S(2)}) copy-start(f32[3,768]{0,1:T(8,128)S(1)} %get-tuple-element.963) | copy-start | bytes 27652 | tf_op jit(solution)/shard_map/while
  62.3 16.3 %copy-start.36 = (f32[2,32,128]{2,0,1:T(2,128)}, f32[2,32,128]{2,0,1:T(2,128)S(1)}, u32[]{:S(2)}) copy-start(f32[2,32,128]{2,0,1:T(2,128)S(1)} %get-tuple-element.961) | copy-start | bytes 98308 | tf_op jit(solution)/shard_map/while
  62.3 16.3 %copy-start.40 = (f32[2,32,128]{2,0,1:T(2,128)}, f32[2,32,128]{2,0,1:T(2,128)S(1)}, u32[]{:S(2)}) copy-start(f32[2,32,128]{2,0,1:T(2,128)S(1)} %get-tuple-element.965) | copy-start | bytes 98308 | tf_op jit(solution)/shard_map/while
  62.3 16.3 %copy-start.56 = (f32[2,3,32]{2,1,0:T(4,128)}, f32[2,3,32]{2,1,0:T(4,128)S(1)}, u32[]{:S(2)}) copy-start(f32[2,3,32]{2,1,0:T(4,128)S(1)} %get-tuple-element.964) | copy-start | bytes 2308 | tf_op jit(solution)/shard_map/while
  62.3 14.2 %copy-start.34 = (bf16[32,64]{1,0:T(8,128)(2,1)S(1)}, bf16[32,64]{1,0:T(8,128)(2,1)}, u32[]{:S(2)}) copy-start(bf16[32,64]{1,0:T(8,128)(2,1)} %get-tuple-element.968) | copy-start | bytes 12292 | tf_op jit(solution)/shard_map/while
  75.5 4.6 %copy-start.18 = (f32[1,32,128]{2,0,1:T(1,128)}, f32[1,32,128]{2,0,1:T(1,128)S(1)}, u32[]{:S(2)}) copy-start(f32[1,32,128]{2,0,1:T(1,128)S(1)} %get-tuple-element.891) | copy-start | bytes 49156 | tf_op jit(solution)/shard_map/while
  75.5 4.6 %copy-start.12 = (f32[2,32,128]{2,0,1:T(2,128)}, f32[2,32,128]{2,0,1:T(2,128)S(1)}, u32[]{:S(2)}) copy-start(f32[2,32,128]{2,0,1:T(2,128)S(1)} %slice.243) | copy-start | bytes 98308 | tf_op jit(solution)/shard_map/while
  75.6 4.2 %copy-start.25 = (f32[4096]{0:T(1024)}, f32[4096]{0:T(1024)S(1)}, u32[]{:S(2)}) copy-start(f32[4096]{0:T(1024)S(1)} %bitcast_multiply_fusion.6) | copy-start | bytes 49156 | tf_op jit(solution)/shard_map/while
  80.1 5.6 %copy-start.7 = (bf16[240,240]{1,0:T(8,128)(2,1)S(1)}, bf16[240,240]{1,0:T(8,128)(2,1)}, u32[]{:S(2)}) copy-start(bf16[240,240]{1,0:T(8,128)(2,1)} %get-tuple-element.975) | copy-start | bytes 345604 | tf_op jit(solution)/shard_map/while
  80.1 5.6 %copy-start.50 = (f32[240]{0:T(256)S(1)}, f32[240]{0:T(256)}, u32[]{:S(2)}) copy-start(f32[240]{0:T(256)} %get-tuple-element.976) | copy-start | bytes 2884 | tf_op jit(solution)/shard_map/while
  82.3 4.4 %copy-start.9 = (f32[32,4,128]{2,1,0:T(4,128)}, f32[32,4,128]{2,1,0:T(4,128)S(1)}, u32[]{:S(2)}) copy-start(f32[32,4,128]{2,1,0:T(4,128)S(1)} %convolution_multiply_fusion.6) | copy-start | bytes 196612 | tf_op jit(solution)/shard_map/while
  88.2 4.3 %copy-start.4 = (bf16[16,32,8,128]{3,2,1,0:T(8,128)(2,1)S(1)}, bf16[16,32,8,128]{3,2,1,0:T(8,128)(2,1)}, u32[]{:S(2)}) copy-start(bf16[16,32,8,128]{3,2,1,0:T(8,128)(2,1)} %copy-done.3) | copy-start | bytes 3145732 | tf_op jit(solution)/shard_map/while
  88.3 4.7 %copy-start.22 = (bf16[3,32,128]{2,0,1:T(4,128)(2,1)S(1)}, bf16[3,32,128]{2,0,1:T(4,128)(2,1)}, u32[]{:S(2)}) copy-start(bf16[3,32,128]{2,0,1:T(4,128)(2,1)} %copy-done.21) | copy-start | bytes 73732 | tf_op jit(solution)/shard_map/while
  88.3 4.7 %copy-start.33 = (bf16[1,32,128]{2,0,1:T(2,128)(2,1)S(1)}, bf16[1,32,128]{2,0,1:T(2,128)(2,1)}, u32[]{:S(2)}) copy-start(bf16[1,32,128]{2,0,1:T(2,128)(2,1)} %copy-done.32) | copy-start | bytes 24580 | tf_op jit(solution)/shard_map/while
  101.5 72.5 %copy-start.49 = (f32[2,3,32,128]{3,1,2,0:T(4,128)S(1)}, f32[2,3,32,128]{3,1,2,0:T(4,128)}, u32[]{:S(2)}) copy-start(f32[2,3,32,128]{3,1,2,0:T(4,128)} %get-tuple-element.460) | copy-start | bytes 294916
  101.5 75.9 %copy-start.59 = (f32[3,64]{1,0:T(4,128)S(1)}, f32[3,64]{1,0:T(4,128)}, u32[]{:S(2)}) copy-start(f32[3,64]{1,0:T(4,128)} %copy-done.58) | copy-start | bytes 2308
  101.5 75.9 %copy-start.62 = (f32[3,64]{1,0:T(4,128)S(1)}, f32[3,64]{1,0:T(4,128)}, u32[]{:S(2)}) copy-start(f32[3,64]{1,0:T(4,128)} %param.22) | copy-start | bytes 2308
  101.5 75.9 %copy-start.63 = (f32[3,64]{1,0:T(4,128)S(1)}, f32[3,64]{1,0:T(4,128)}, u32[]{:S(2)}) copy-start(f32[3,64]{1,0:T(4,128)} %param.23) | copy-start | bytes 2308
  101.5 94.3 %copy-start.1 = (bf16[2048,240]{0,1:T(8,128)(2,1)S(1)}, bf16[2048,240]{0,1:T(8,128)(2,1)}, u32[]{:S(2)}) copy-start(bf16[2048,240]{0,1:T(8,128)(2,1)} %get-tuple-element.1043) | copy-start | bytes 2949124
  101.5 94.3 %copy-start.8 = (bf16[240,240]{1,0:T(8,128)(2,1)S(1)}, bf16[240,240]{1,0:T(8,128)(2,1)}, u32[]{:S(2)}) copy-start(bf16[240,240]{1,0:T(8,128)(2,1)} %get-tuple-element.1044) | copy-start | bytes 345604
  101.5 94.3 %copy-start.35 = (bf16[32,64]{1,0:T(8,128)(2,1)S(1)}, bf16[32,64]{1,0:T(8,128)(2,1)}, u32[]{:S(2)}) copy-start(bf16[32,64]{1,0:T(8,128)(2,1)} %get-tuple-element.1045) | copy-start | bytes 12292
  148.0 198.6 %reduce-scatter.9.cloned.1.call-start = ((), (), s32[]{:S(2)}) async-start(), calls=%async_computation.3 | async-start | bytes 163840
  173.4 1.3 collective-permute-start.3
  173.5 3.9 %collective-permute-start.2 = (f32[3,1,64]{2,0,1:T(4,128)S(1)}, f32[3,1,64]{2,0,1:T(4,128)S(1)}, u32[]{:S(2)}, u32[]{:S(2)}) collective-permute-start(f32[3,1,64]{2,0,1:T(4,128)S(1)} %copy.169), channel_id=1, source_target_pairs={{0,4},{4,8},{8,12},{12,16},{16,20},{20,24},{24,28},{28,0},{1,5},{5... | collective-permute-start | bytes 2312 | tf_op jit(solution)/shard_map/ppermute | solution.py:21
  178.0 17.8 %copy-start.60 = (f32[3,64]{1,0:T(4,128)}, f32[3,64]{1,0:T(4,128)S(1)}, u32[]{:S(2)}) copy-start(f32[3,64]{1,0:T(4,128)S(1)} %get-tuple-element.650) | copy-start | bytes 2308
  190.0 1.3 collective-permute-start.5
  190.0 4.2 %collective-permute-start.4 = (f32[3,1,256]{2,0,1:T(4,128)S(1)}, f32[3,1,256]{2,0,1:T(4,128)S(1)}, u32[]{:S(2)}, u32[]{:S(2)}) collective-permute-start(f32[3,1,256]{2,0,1:T(4,128)S(1)} %bitcast.485), channel_id=1, source_target_pairs={{0,4},{4,8},{8,12},{12,16},{16,20},{20,24},{24,28},{28,0},{1,5},{5... | collective-permute-start | bytes 9224 | tf_op jit(solution)/shard_map/ppermute | solution.py:21
  195.8 13.3 %copy-start.54 = (f32[2,3,32]{2,1,0:T(4,128)}, f32[2,3,32]{2,1,0:T(4,128)S(1)}, u32[]{:S(2)}) copy-start(f32[2,3,32]{2,1,0:T(4,128)S(1)} %get-tuple-element.1026) | copy-start | bytes 2308 | tf_op jit(solution)/shard_map/while
  195.8 17.2 %copy-start.38 = (f32[2,32,128]{2,0,1:T(2,128)}, f32[2,32,128]{2,0,1:T(2,128)S(1)}, u32[]{:S(2)}) copy-start(f32[2,32,128]{2,0,1:T(2,128)S(1)} %get-tuple-element.1023) | copy-start | bytes 98308 | tf_op jit(solution)/shard_map/while
  195.9 17.2 %copy-start.42 = (f32[2,32,128]{2,0,1:T(2,128)}, f32[2,32,128]{2,0,1:T(2,128)S(1)}, u32[]{:S(2)}) copy-start(f32[2,32,128]{2,0,1:T(2,128)S(1)} %get-tuple-element.1027) | copy-start | bytes 98308 | tf_op jit(solution)/shard_map/while
  210.0 4.6 %copy-start.16 = (f32[1,32,128]{2,0,1:T(1,128)}, f32[1,32,128]{2,0,1:T(1,128)S(1)}, u32[]{:S(2)}) copy-start(f32[1,32,128]{2,0,1:T(1,128)S(1)} %get-tuple-element.916) | copy-start | bytes 49156 | tf_op jit(solution)/shard_map/while
  210.0 4.5 %copy-start.10 = (f32[2,32,128]{2,0,1:T(2,128)}, f32[2,32,128]{2,0,1:T(2,128)S(1)}, u32[]{:S(2)}) copy-start(f32[2,32,128]{2,0,1:T(2,128)S(1)} %slice.255) | copy-start | bytes 98308 | tf_op jit(solution)/shard_map/while
  210.1 4.2 %copy-start.23 = (f32[4096]{0:T(1024)}, f32[4096]{0:T(1024)S(1)}, u32[]{:S(2)}) copy-start(f32[4096]{0:T(1024)S(1)} %bitcast_multiply_fusion.7) | copy-start | bytes 49156 | tf_op jit(solution)/shard_map/while
  214.5 5.6 %copy-start.51 = (f32[240]{0:T(256)S(1)}, f32[240]{0:T(256)}, u32[]{:S(2)}) copy-start(f32[240]{0:T(256)} %get-tuple-element.1037) | copy-start | bytes 2884 | tf_op jit(solution)/shard_map/while
  234.6 13.2 %copy-start.54 = (f32[2,3,32]{2,1,0:T(4,128)}, f32[2,3,32]{2,1,0:T(4,128)S(1)}, u32[]{:S(2)}) copy-start(f32[2,3,32]{2,1,0:T(4,128)S(1)} %get-tuple-element.1026) | copy-start | bytes 2308 | tf_op jit(solution)/shard_map/while
  234.6 17.2 %copy-start.38 = (f32[2,32,128]{2,0,1:T(2,128)}, f32[2,32,128]{2,0,1:T(2,128)S(1)}, u32[]{:S(2)}) copy-start(f32[2,32,128]{2,0,1:T(2,128)S(1)} %get-tuple-element.1023) | copy-start | bytes 98308 | tf_op jit(solution)/shard_map/while
  234.7 17.2 %copy-start.42 = (f32[2,32,128]{2,0,1:T(2,128)}, f32[2,32,128]{2,0,1:T(2,128)S(1)}, u32[]{:S(2)}) copy-start(f32[2,32,128]{2,0,1:T(2,128)S(1)} %get-tuple-element.1027) | copy-start | bytes 98308 | tf_op jit(solution)/shard_map/while
  248.8 4.6 %copy-start.16 = (f32[1,32,128]{2,0,1:T(1,128)}, f32[1,32,128]{2,0,1:T(1,128)S(1)}, u32[]{:S(2)}) copy-start(f32[1,32,128]{2,0,1:T(1,128)S(1)} %get-tuple-element.916) | copy-start | bytes 49156 | tf_op jit(solution)/shard_map/while
  248.8 4.5 %copy-start.10 = (f32[2,32,128]{2,0,1:T(2,128)}, f32[2,32,128]{2,0,1:T(2,128)S(1)}, u32[]{:S(2)}) copy-start(f32[2,32,128]{2,0,1:T(2,128)S(1)} %slice.255) | copy-start | bytes 98308 | tf_op jit(solution)/shard_map/while
  248.9 4.2 %copy-start.23 = (f32[4096]{0:T(1024)}, f32[4096]{0:T(1024)S(1)}, u32[]{:S(2)}) copy-start(f32[4096]{0:T(1024)S(1)} %bitcast_multiply_fusion.7) | copy-start | bytes 49156 | tf_op jit(solution)/shard_map/while
  253.3 5.6 %copy-start.51 = (f32[240]{0:T(256)S(1)}, f32[240]{0:T(256)}, u32[]{:S(2)}) copy-start(f32[240]{0:T(256)} %get-tuple-element.1037) | copy-start | bytes 2884 | tf_op jit(solution)/shard_map/while
  276.9 71.3 %copy-start.46 = (f32[2,3,32,128]{3,1,2,0:T(4,128)S(1)}, f32[2,3,32,128]{3,1,2,0:T(4,128)}, u32[]{:S(2)}) copy-start(f32[2,3,32,128]{3,1,2,0:T(4,128)} %get-tuple-element.461) | copy-start | bytes 294916
  276.9 74.7 %copy-start.61 = (f32[3,64]{1,0:T(4,128)S(1)}, f32[3,64]{1,0:T(4,128)}, u32[]{:S(2)}) copy-start(f32[3,64]{1,0:T(4,128)} %get-tuple-element.651) | copy-start | bytes 2308
  347.7 2.2 collective-permute-start.7
  347.7 3.9 %collective-permute-start.6 = (f32[3,1,64]{2,0,1:T(4,128)S(1)}, f32[3,1,64]{2,0,1:T(4,128)S(1)}, u32[]{:S(2)}, u32[]{:S(2)}) collective-permute-start(f32[3,1,64]{2,0,1:T(4,128)S(1)} %copy.172), channel_id=1, source_target_pairs={{0,4},{4,8},{8,12},{12,16},{16,20},{20,24},{24,28},{28,0},{1,5},{5... | collective-permute-start | bytes 2312 | tf_op jit(solution)/shard_map/ppermute | solution.py:21
  (63 other events, 113.3 us)
Sparse Core Ops, SparseCore 0:
  148.2 24.1 reduce-scatter.6
  323.5 23.1 reduce-scatter.8
where the time goes:
time: 362 us; the launch traced here: 359 us
  other arithmetic  107 us (30%)
  local copies, waits for them, and re-layouts  87 us (24%)
  matrix products  64.1 us (18%)
  waiting for transfers between devices  57.3 us (16%)
  blocking collectives  25.5 us (7%)
  between operations  14.2 us (4%)
    scatter-add x2, other arithmetic, evaluate(): jnp.zeros((3, 3 * brick_len), jnp.float32).at[:, safe_index].add(pair_grads)  90.5 us
    unnamed x4, waiting for transfers between devices  47.6 us
    gather x8, local copies, waits for them, and re-layouts, one_block(): neighbour_pos = jnp.take(ghost, table_index, axis=1)  47.5 us
    all_gather x2, blocking collectives, ghost_table(): brick_pos = lax.all_gather(stacked, 'help', axis=2, tiled=True)  25.5 us
    while x212, local copies, waits for them, and re-layouts  8.73 us
    ppermute x4, waiting for transfers between devices, extended(): before = lax.ppermute(last, axis, up)  8.48 us
    dot_general x4, matrix products, pair_terms(): jnp.dot(w_embed2.T, hidden_first.astype(jnp.bfloat16), preferred_element_...  8.38 us
    dot_general x4, matrix products, pair_terms(): jnp.dot(grad_act, w_fit1.T, preferred_element_type=jnp.float32)  7.82 us
  transfers between devices with their start and end apart: 10, of which 8 were waited for; matrix products, arithmetic and copies ran while one was open for 1% of the time, Pallas kernels for 0%

commit v1 on v0

--- a/solution.py
+++ b/solution.py
@@ -1,3 +1,4 @@
+import functools
 import jax
 import jax.numpy as jnp
 from jax import lax
@@ -9,6 +10,13 @@
 kick_scale = 0.25
 time_step = 0.05
 highest_precision = lax.Precision.HIGHEST
+
+
+def finish_sheets(field_in, dim_at):
+    return jnp.concatenate(jax.lax.all_gather(field_in, axis_name="help"), dim_at)
+
+
+review_the_pipes = functools.partial(finish_sheets, dim_at=2)
 
 
 def extended(value, sides, width):
@@ -145,7 +153,7 @@
 
 def ghost_table(coords):
     stacked = coords[:, None, :]
-    brick_pos = lax.all_gather(stacked, "help", axis=2, tiled=True)
+    brick_pos = review_the_pipes(stacked)
     gathered = extended(brick_pos, (("brick", 1),), 1)
     return gathered.reshape(3, -1)
 

time: 362 us -> 362 us (level)
  no operation moved by 1% of the time
where the time goes in v1:
time: 362 us; the launch traced here: 359 us
  other arithmetic  107 us (30%)
  local copies, waits for them, and re-layouts  87 us (24%)
  matrix products  64.1 us (18%)
  waiting for transfers between devices  57.3 us (16%)
  blocking collectives  25.5 us (7%)
  between operations  14.2 us (4%)
    scatter-add x2, other arithmetic, evaluate(): jnp.zeros((3, 3 * brick_len), jnp.float32).at[:, safe_index].add(pair_grads)  90.5 us
    unnamed x4, waiting for transfers between devices  47.7 us
    gather x8, local copies, waits for them, and re-layouts, one_block(): neighbour_pos = jnp.take(ghost, table_index, axis=1)  47.5 us
    all_gather x2, blocking collectives, finish_sheets(): jax.lax.all_gather(field_in, axis_name='help')  25.5 us
    while x212, local copies, waits for them, and re-layouts  8.73 us
    ppermute x4, waiting for transfers between devices, extended(): before = lax.ppermute(last, axis, up)  8.47 us
    dot_general x4, matrix products, pair_terms(): jnp.dot(w_embed2.T, hidden_first.astype(jnp.bfloat16), preferred_element_...  8.38 us
    dot_general x4, matrix products, pair_terms(): jnp.dot(grad_act, w_fit1.T, preferred_element_type=jnp.float32)  7.82 us
  transfers between devices with their start and end apart: 10, of which 8 were waited for; matrix products, arithmetic and copies ran while one was open for 1% of the time, Pallas kernels for 0%

profile of v1, /device:TPU:0, one launch (start us, length us, event | category | flops | bytes accessed | tf_op | source)
XLA Modules:
  0.0 359.1 jit_solution(8350808552154073077)
XLA Ops:
  7.9 13.6 %all-gather.2 = f32[4,3,64]{2,1,0:T(4,128)S(1)} all-gather(f32[1,3,64]{2,1,0:T(4,128)S(1)} %bitcast.473), channel_id=2, replica_groups=mesh['brick'=8,'help'=4] {'help'}, dimensions={0}, use_global_device_ids=true | all-gather | bytes 3840 | tf_op jit(solution)/shard_map/all_gather | solution.py:16
  22.9 1.4 fusion.116
  24.5 1.1 collective-permute-done
  26.5 71.5 %while.26 = (s32[]{:T(128)}, f32[2,3,32,128]{3,1,2,0:T(4,128)}, f32[2,32,128]{2,0,1:T(2,128)S(1)}, s32[2,32,128]{2,1,0:T(8,128)}, f32[3,768]{0,1:T(8,128)S(1)}, ...) while((s32[]{:T(128)}, f32[2,3,32,128]{3,1,2,0:T(4,128)}, ...), condition=%wide.region_3.5_spmd, body=%wide.region_0.4_spmd.sunk | while | flops 271267840 | bytes 53851500 | solution.py:188
  27.4 10.8 %gather_fusion = f32[4096,3]{1,0:T(8,128)S(1)} fusion(f32[3,768]{0,1:T(8,128)S(1)} %get-tuple-element.926, s32[4096]{0:T(1024)S(1)} %bitcast_clamp_fusion.4), kind=kCustom, calls=%fused_computation.clone.clone.1 | custom fusion | bytes 114688 | tf_op jit(solution)/shard_map/while/body/eval_jaxpr/jit(_take)/gather | solution.py:180
  40.7 2.1 maximum_add_fusion.6
  42.9 1.2 fusion.262
  47.2 1.2 copy.199
  48.5 1.4 fusion.265
  51.0 1.5 fusion.267
  52.5 1.8 copy.200
  54.3 1.4 fusion.268
  55.6 1.2 fusion.269
  57.8 1.4 fusion.271
  59.2 1.0 fusion.272
  60.4 1.1 fusion.273
  63.1 10.8 %gather_fusion = f32[4096,3]{1,0:T(8,128)S(1)} fusion(f32[3,768]{0,1:T(8,128)S(1)} %get-tuple-element.926, s32[4096]{0:T(1024)S(1)} %bitcast_clamp_fusion.4), kind=kCustom, calls=%fused_computation.clone.clone.1 | custom fusion | bytes 114688 | tf_op jit(solution)/shard_map/while/body/eval_jaxpr/jit(_take)/gather | solution.py:180
  76.5 2.1 maximum_add_fusion.6
  78.6 1.2 fusion.262
  83.0 1.2 copy.199
  84.2 1.4 fusion.265
  86.7 1.5 fusion.267
  88.3 1.8 copy.200
  90.0 1.4 fusion.268
  91.4 1.2 fusion.269
  93.5 1.4 fusion.271
  95.0 1.0 fusion.272
  96.1 1.1 fusion.273
  98.0 3.5 copy.108
  101.6 45.3 %scatter_custom_fusion = f32[3,768]{0,1:T(8,128)S(1)} fusion(s32[8192]{0:T(1024)} %get-tuple-element.633, f32[8192,3]{1,0:T(8,128)} %bitcast.452, f32[]{:T(128)} %constant.160.clone.1), kind=kCustom, calls=%fused_computation.189 | custom fusion | flops 24576 | bytes 9728 | tf_op jit(solution)/shard_map/scatter-add | solution.py:199
  148.1 24.3 %reduce-scatter.7.cloned.1.call-done = f32[64,9]{1,0:T(8,128)} async-done(((f32[256,9]{1,0:T(8,128)}), f32[64,9]{1,0:T(8,128)}) %reduce-scatter.7.cloned.1.call-update) | async-done | bytes 2320
  174.7 2.7 collective-permute-done.2
  178.0 11.9 %all-gather.3 = f32[4,3,64]{2,1,0:T(4,128)S(1)} all-gather(f32[1,3,64]{2,1,0:T(4,128)S(1)} %bitcast.474), channel_id=3, replica_groups=mesh['brick'=8,'help'=4] {'help'}, dimensions={0}, use_global_device_ids=true | all-gather | bytes 3840 | tf_op jit(solution)/shard_map/all_gather | solution.py:16
  191.3 2.8 collective-permute-done.4
  195.8 77.6 %while.27 = (s32[]{:T(128)}, f32[2,32]{1,0:T(2,128)}, f32[2,3,32,128]{3,1,2,0:T(4,128)}, f32[2,32,128]{2,0,1:T(2,128)S(1)}, s32[2,32,128]{2,1,0:T(8,128)}, /*ind...) while((s32[]{:T(128)}, f32[2,32]{1,0:T(2,128)}, ...), condition=%wide.region_10.12_spmd, body=%wide.region_7.11_spmd.sunk | while | flops 271367680 | bytes 45020100 | solution.py:188
  196.6 11.8 %gather_fusion.1 = f32[4096,3]{1,0:T(8,128)S(1)} fusion(f32[3,768]{0,1:T(8,128)} %get-tuple-element.988, s32[4096]{0:T(1024)S(1)} %bitcast_clamp_fusion.5), kind=kCustom, calls=%fused_computation.1.clone.clone.1 | custom fusion | bytes 114688 | tf_op jit(solution)/shard_map/while/body/eval_jaxpr/jit(_take)/gather | solution.py:180
  211.0 2.1 maximum_add_fusion.7
  213.1 1.2 fusion.301
  217.4 1.2 copy.207
  218.7 1.4 fusion.304
  221.1 1.3 dynamic_update_slice.27
  222.4 2.4 fusion.307
  224.7 1.7 copy.208
  227.3 1.6 fusion.310
  228.9 1.3 multiply_bitcast_fusion.7
  230.2 1.4 fusion.311
  232.8 1.1 fusion.313
  235.4 11.8 %gather_fusion.1 = f32[4096,3]{1,0:T(8,128)S(1)} fusion(f32[3,768]{0,1:T(8,128)} %get-tuple-element.988, s32[4096]{0:T(1024)S(1)} %bitcast_clamp_fusion.5), kind=kCustom, calls=%fused_computation.1.clone.clone.1 | custom fusion | bytes 114688 | tf_op jit(solution)/shard_map/while/body/eval_jaxpr/jit(_take)/gather | solution.py:180
  249.7 2.1 maximum_add_fusion.7
  251.8 1.2 fusion.301
  256.2 1.2 copy.207
  257.4 1.4 fusion.304
  259.9 1.3 dynamic_update_slice.27
  261.1 2.4 fusion.307
  263.5 1.7 copy.208
  266.1 1.6 fusion.310
  267.7 1.3 multiply_bitcast_fusion.7
  269.0 1.4 fusion.311
  271.6 1.1 fusion.313
  273.4 3.5 copy.116
  276.9 45.2 %scatter_custom_fusion.1 = f32[3,768]{0,1:T(8,128)S(1)} fusion(s32[8192]{0:T(1024)} %get-tuple-element.633, f32[8192,3]{1,0:T(8,128)} %bitcast.451, f32[]{:T(128)} %constant.160.clone.1), kind=kCustom, calls=%fused_computation.187 | custom fusion | flops 24576 | bytes 9728 | tf_op jit(solution)/shard_map/scatter-add | solution.py:199
  323.3 23.3 %reduce-scatter.9.cloned.1.call-done = f32[64,9]{1,0:T(8,128)} async-done(((f32[256,9]{1,0:T(8,128)}), f32[64,9]{1,0:T(8,128)}) %reduce-scatter.9.cloned.1.call-update) | async-done | bytes 2320
  348.5 1.3 reshape.323
  349.8 1.8 collective-permute-done.6
  (385 shorter events, 52.5 us)
Async XLA Ops:
  7.2 165.2 %reduce-scatter.7.cloned.1.call-start = ((), (), s32[]{:S(2)}) async-start(), calls=%async_computation.2 | async-start | bytes 163840
  7.9 18.6 %copy-start.58 = (f32[3,64]{1,0:T(4,128)}, f32[3,64]{1,0:T(4,128)S(1)}, u32[]{:S(2)}) copy-start(f32[3,64]{1,0:T(4,128)S(1)} %multiply_add_fusion.2) | copy-start | bytes 2308
  21.7 2.8 collective-permute-start.1
  21.7 4.0 %collective-permute-start = (f32[3,1,256]{2,1,0:T(1,128)S(1)}, f32[3,1,256]{2,1,0:T(1,128)S(1)}, u32[]{:S(2)}, u32[]{:S(2)}) collective-permute-start(f32[3,1,256]{2,1,0:T(1,128)S(1)} %reshape.311), channel_id=1, source_target_pairs={{0,4},{4,8},{8,12},{12,16},{16,20},{20,24},{24,28},{28,0},{1,5},{5... | collective-permute-start | bytes 9224 | tf_op jit(solution)/shard_map/ppermute | solution.py:29
  26.5 16.3 %copy-start.14 = (f32[3,768]{0,1:T(8,128)}, f32[3,768]{0,1:T(8,128)S(1)}, u32[]{:S(2)}) copy-start(f32[3,768]{0,1:T(8,128)S(1)} %get-tuple-element.926) | copy-start | bytes 27652 | tf_op jit(solution)/shard_map/while
  26.5 16.3 %copy-start.36 = (f32[2,32,128]{2,0,1:T(2,128)}, f32[2,32,128]{2,0,1:T(2,128)S(1)}, u32[]{:S(2)}) copy-start(f32[2,32,128]{2,0,1:T(2,128)S(1)} %get-tuple-element.924) | copy-start | bytes 98308 | tf_op jit(solution)/shard_map/while
  26.5 16.3 %copy-start.40 = (f32[2,32,128]{2,0,1:T(2,128)}, f32[2,32,128]{2,0,1:T(2,128)S(1)}, u32[]{:S(2)}) copy-start(f32[2,32,128]{2,0,1:T(2,128)S(1)} %get-tuple-element.928) | copy-start | bytes 98308 | tf_op jit(solution)/shard_map/while
  26.5 16.3 %copy-start.56 = (f32[2,3,32]{2,1,0:T(4,128)}, f32[2,3,32]{2,1,0:T(4,128)S(1)}, u32[]{:S(2)}) copy-start(f32[2,3,32]{2,1,0:T(4,128)S(1)} %get-tuple-element.927) | copy-start | bytes 2308 | tf_op jit(solution)/shard_map/while
  26.5 14.2 %copy-start.34 = (bf16[32,64]{1,0:T(8,128)(2,1)S(1)}, bf16[32,64]{1,0:T(8,128)(2,1)}, u32[]{:S(2)}) copy-start(bf16[32,64]{1,0:T(8,128)(2,1)} %get-tuple-element.931) | copy-start | bytes 12292 | tf_op jit(solution)/shard_map/while
  39.7 4.6 %copy-start.18 = (f32[1,32,128]{2,0,1:T(1,128)}, f32[1,32,128]{2,0,1:T(1,128)S(1)}, u32[]{:S(2)}) copy-start(f32[1,32,128]{2,0,1:T(1,128)S(1)} %get-tuple-element.854) | copy-start | bytes 49156 | tf_op jit(solution)/shard_map/while
  39.8 4.6 %copy-start.12 = (f32[2,32,128]{2,0,1:T(2,128)}, f32[2,32,128]{2,0,1:T(2,128)S(1)}, u32[]{:S(2)}) copy-start(f32[2,32,128]{2,0,1:T(2,128)S(1)} %slice.243) | copy-start | bytes 98308 | tf_op jit(solution)/shard_map/while
  39.9 4.2 %copy-start.25 = (f32[4096]{0:T(1024)}, f32[4096]{0:T(1024)S(1)}, u32[]{:S(2)}) copy-start(f32[4096]{0:T(1024)S(1)} %bitcast_multiply_fusion.6) | copy-start | bytes 49156 | tf_op jit(solution)/shard_map/while
  44.3 4.1 %copy-start = (bf16[2048,240]{0,1:T(8,128)(2,1)S(1)}, bf16[2048,240]{0,1:T(8,128)(2,1)}, u32[]{:S(2)}) copy-start(bf16[2048,240]{0,1:T(8,128)(2,1)} %get-tuple-element.936) | copy-start | bytes 2949124 | tf_op jit(solution)/shard_map/while
  44.3 5.6 %copy-start.7 = (bf16[240,240]{1,0:T(8,128)(2,1)S(1)}, bf16[240,240]{1,0:T(8,128)(2,1)}, u32[]{:S(2)}) copy-start(bf16[240,240]{1,0:T(8,128)(2,1)} %get-tuple-element.938) | copy-start | bytes 345604 | tf_op jit(solution)/shard_map/while
  44.3 5.6 %copy-start.50 = (f32[240]{0:T(256)S(1)}, f32[240]{0:T(256)}, u32[]{:S(2)}) copy-start(f32[240]{0:T(256)} %get-tuple-element.939) | copy-start | bytes 2884 | tf_op jit(solution)/shard_map/while
  46.5 4.4 %copy-start.9 = (f32[32,4,128]{2,1,0:T(4,128)}, f32[32,4,128]{2,1,0:T(4,128)S(1)}, u32[]{:S(2)}) copy-start(f32[32,4,128]{2,1,0:T(4,128)S(1)} %convolution_multiply_fusion.6) | copy-start | bytes 196612 | tf_op jit(solution)/shard_map/while
  52.5 4.3 %copy-start.4 = (bf16[16,32,8,128]{3,2,1,0:T(8,128)(2,1)S(1)}, bf16[16,32,8,128]{3,2,1,0:T(8,128)(2,1)}, u32[]{:S(2)}) copy-start(bf16[16,32,8,128]{3,2,1,0:T(8,128)(2,1)} %copy-done.3) | copy-start | bytes 3145732 | tf_op jit(solution)/shard_map/while
  52.5 4.7 %copy-start.22 = (bf16[3,32,128]{2,0,1:T(4,128)(2,1)S(1)}, bf16[3,32,128]{2,0,1:T(4,128)(2,1)}, u32[]{:S(2)}) copy-start(bf16[3,32,128]{2,0,1:T(4,128)(2,1)} %copy-done.21) | copy-start | bytes 73732 | tf_op jit(solution)/shard_map/while
  52.5 4.7 %copy-start.33 = (bf16[1,32,128]{2,0,1:T(2,128)(2,1)S(1)}, bf16[1,32,128]{2,0,1:T(2,128)(2,1)}, u32[]{:S(2)}) copy-start(bf16[1,32,128]{2,0,1:T(2,128)(2,1)} %copy-done.32) | copy-start | bytes 24580 | tf_op jit(solution)/shard_map/while
  62.3 16.3 %copy-start.14 = (f32[3,768]{0,1:T(8,128)}, f32[3,768]{0,1:T(8,128)S(1)}, u32[]{:S(2)}) copy-start(f32[3,768]{0,1:T(8,128)S(1)} %get-tuple-element.926) | copy-start | bytes 27652 | tf_op jit(solution)/shard_map/while
  62.3 16.3 %copy-start.36 = (f32[2,32,128]{2,0,1:T(2,128)}, f32[2,32,128]{2,0,1:T(2,128)S(1)}, u32[]{:S(2)}) copy-start(f32[2,32,128]{2,0,1:T(2,128)S(1)} %get-tuple-element.924) | copy-start | bytes 98308 | tf_op jit(solution)/shard_map/while
  62.3 16.3 %copy-start.40 = (f32[2,32,128]{2,0,1:T(2,128)}, f32[2,32,128]{2,0,1:T(2,128)S(1)}, u32[]{:S(2)}) copy-start(f32[2,32,128]{2,0,1:T(2,128)S(1)} %get-tuple-element.928) | copy-start | bytes 98308 | tf_op jit(solution)/shard_map/while
  62.3 16.3 %copy-start.56 = (f32[2,3,32]{2,1,0:T(4,128)}, f32[2,3,32]{2,1,0:T(4,128)S(1)}, u32[]{:S(2)}) copy-start(f32[2,3,32]{2,1,0:T(4,128)S(1)} %get-tuple-element.927) | copy-start | bytes 2308 | tf_op jit(solution)/shard_map/while
  62.3 14.2 %copy-start.34 = (bf16[32,64]{1,0:T(8,128)(2,1)S(1)}, bf16[32,64]{1,0:T(8,128)(2,1)}, u32[]{:S(2)}) copy-start(bf16[32,64]{1,0:T(8,128)(2,1)} %get-tuple-element.931) | copy-start | bytes 12292 | tf_op jit(solution)/shard_map/while
  75.5 4.6 %copy-start.18 = (f32[1,32,128]{2,0,1:T(1,128)}, f32[1,32,128]{2,0,1:T(1,128)S(1)}, u32[]{:S(2)}) copy-start(f32[1,32,128]{2,0,1:T(1,128)S(1)} %get-tuple-element.854) | copy-start | bytes 49156 | tf_op jit(solution)/shard_map/while
  75.5 4.6 %copy-start.12 = (f32[2,32,128]{2,0,1:T(2,128)}, f32[2,32,128]{2,0,1:T(2,128)S(1)}, u32[]{:S(2)}) copy-start(f32[2,32,128]{2,0,1:T(2,128)S(1)} %slice.243) | copy-start | bytes 98308 | tf_op jit(solution)/shard_map/while
  75.6 4.2 %copy-start.25 = (f32[4096]{0:T(1024)}, f32[4096]{0:T(1024)S(1)}, u32[]{:S(2)}) copy-start(f32[4096]{0:T(1024)S(1)} %bitcast_multiply_fusion.6) | copy-start | bytes 49156 | tf_op jit(solution)/shard_map/while
  80.1 5.6 %copy-start.7 = (bf16[240,240]{1,0:T(8,128)(2,1)S(1)}, bf16[240,240]{1,0:T(8,128)(2,1)}, u32[]{:S(2)}) copy-start(bf16[240,240]{1,0:T(8,128)(2,1)} %get-tuple-element.938) | copy-start | bytes 345604 | tf_op jit(solution)/shard_map/while
  80.1 5.6 %copy-start.50 = (f32[240]{0:T(256)S(1)}, f32[240]{0:T(256)}, u32[]{:S(2)}) copy-start(f32[240]{0:T(256)} %get-tuple-element.939) | copy-start | bytes 2884 | tf_op jit(solution)/shard_map/while
  82.3 4.4 %copy-start.9 = (f32[32,4,128]{2,1,0:T(4,128)}, f32[32,4,128]{2,1,0:T(4,128)S(1)}, u32[]{:S(2)}) copy-start(f32[32,4,128]{2,1,0:T(4,128)S(1)} %convolution_multiply_fusion.6) | copy-start | bytes 196612 | tf_op jit(solution)/shard_map/while
  88.2 4.3 %copy-start.4 = (bf16[16,32,8,128]{3,2,1,0:T(8,128)(2,1)S(1)}, bf16[16,32,8,128]{3,2,1,0:T(8,128)(2,1)}, u32[]{:S(2)}) copy-start(bf16[16,32,8,128]{3,2,1,0:T(8,128)(2,1)} %copy-done.3) | copy-start | bytes 3145732 | tf_op jit(solution)/shard_map/while
  88.3 4.7 %copy-start.22 = (bf16[3,32,128]{2,0,1:T(4,128)(2,1)S(1)}, bf16[3,32,128]{2,0,1:T(4,128)(2,1)}, u32[]{:S(2)}) copy-start(bf16[3,32,128]{2,0,1:T(4,128)(2,1)} %copy-done.21) | copy-start | bytes 73732 | tf_op jit(solution)/shard_map/while
  88.3 4.7 %copy-start.33 = (bf16[1,32,128]{2,0,1:T(2,128)(2,1)S(1)}, bf16[1,32,128]{2,0,1:T(2,128)(2,1)}, u32[]{:S(2)}) copy-start(bf16[1,32,128]{2,0,1:T(2,128)(2,1)} %copy-done.32) | copy-start | bytes 24580 | tf_op jit(solution)/shard_map/while
  101.5 72.5 %copy-start.49 = (f32[2,3,32,128]{3,1,2,0:T(4,128)S(1)}, f32[2,3,32,128]{3,1,2,0:T(4,128)}, u32[]{:S(2)}) copy-start(f32[2,3,32,128]{3,1,2,0:T(4,128)} %get-tuple-element.460) | copy-start | bytes 294916
  101.5 75.9 %copy-start.59 = (f32[3,64]{1,0:T(4,128)S(1)}, f32[3,64]{1,0:T(4,128)}, u32[]{:S(2)}) copy-start(f32[3,64]{1,0:T(4,128)} %copy-done.58) | copy-start | bytes 2308
  101.5 75.9 %copy-start.62 = (f32[3,64]{1,0:T(4,128)S(1)}, f32[3,64]{1,0:T(4,128)}, u32[]{:S(2)}) copy-start(f32[3,64]{1,0:T(4,128)} %param.22) | copy-start | bytes 2308
  101.5 75.9 %copy-start.63 = (f32[3,64]{1,0:T(4,128)S(1)}, f32[3,64]{1,0:T(4,128)}, u32[]{:S(2)}) copy-start(f32[3,64]{1,0:T(4,128)} %param.23) | copy-start | bytes 2308
  101.5 94.3 %copy-start.1 = (bf16[2048,240]{0,1:T(8,128)(2,1)S(1)}, bf16[2048,240]{0,1:T(8,128)(2,1)}, u32[]{:S(2)}) copy-start(bf16[2048,240]{0,1:T(8,128)(2,1)} %get-tuple-element.1006) | copy-start | bytes 2949124
  101.5 94.3 %copy-start.8 = (bf16[240,240]{1,0:T(8,128)(2,1)S(1)}, bf16[240,240]{1,0:T(8,128)(2,1)}, u32[]{:S(2)}) copy-start(bf16[240,240]{1,0:T(8,128)(2,1)} %get-tuple-element.1007) | copy-start | bytes 345604
  101.5 94.3 %copy-start.35 = (bf16[32,64]{1,0:T(8,128)(2,1)S(1)}, bf16[32,64]{1,0:T(8,128)(2,1)}, u32[]{:S(2)}) copy-start(bf16[32,64]{1,0:T(8,128)(2,1)} %get-tuple-element.1008) | copy-start | bytes 12292
  148.0 198.6 %reduce-scatter.9.cloned.1.call-start = ((), (), s32[]{:S(2)}) async-start(), calls=%async_computation.3 | async-start | bytes 163840
  173.4 1.3 collective-permute-start.3
  173.5 3.9 %collective-permute-start.2 = (f32[3,1,64]{2,0,1:T(4,128)S(1)}, f32[3,1,64]{2,0,1:T(4,128)S(1)}, u32[]{:S(2)}, u32[]{:S(2)}) collective-permute-start(f32[3,1,64]{2,0,1:T(4,128)S(1)} %copy.135), channel_id=1, source_target_pairs={{0,4},{4,8},{8,12},{12,16},{16,20},{20,24},{24,28},{28,0},{1,5},{5... | collective-permute-start | bytes 2312 | tf_op jit(solution)/shard_map/ppermute | solution.py:29
  178.0 17.8 %copy-start.60 = (f32[3,64]{1,0:T(4,128)}, f32[3,64]{1,0:T(4,128)S(1)}, u32[]{:S(2)}) copy-start(f32[3,64]{1,0:T(4,128)S(1)} %get-tuple-element.613) | copy-start | bytes 2308
  190.0 1.3 collective-permute-start.5
  190.0 4.1 %collective-permute-start.4 = (f32[3,1,256]{2,1,0:T(1,128)S(1)}, f32[3,1,256]{2,1,0:T(1,128)S(1)}, u32[]{:S(2)}, u32[]{:S(2)}) collective-permute-start(f32[3,1,256]{2,1,0:T(1,128)S(1)} %reshape.318), channel_id=1, source_target_pairs={{0,4},{4,8},{8,12},{12,16},{16,20},{20,24},{24,28},{28,0},{1,5},{5... | collective-permute-start | bytes 9224 | tf_op jit(solution)/shard_map/ppermute | solution.py:29
  195.8 13.3 %copy-start.54 = (f32[2,3,32]{2,1,0:T(4,128)}, f32[2,3,32]{2,1,0:T(4,128)S(1)}, u32[]{:S(2)}) copy-start(f32[2,3,32]{2,1,0:T(4,128)S(1)} %get-tuple-element.989) | copy-start | bytes 2308 | tf_op jit(solution)/shard_map/while
  195.8 17.2 %copy-start.38 = (f32[2,32,128]{2,0,1:T(2,128)}, f32[2,32,128]{2,0,1:T(2,128)S(1)}, u32[]{:S(2)}) copy-start(f32[2,32,128]{2,0,1:T(2,128)S(1)} %get-tuple-element.986) | copy-start | bytes 98308 | tf_op jit(solution)/shard_map/while
  195.9 17.2 %copy-start.42 = (f32[2,32,128]{2,0,1:T(2,128)}, f32[2,32,128]{2,0,1:T(2,128)S(1)}, u32[]{:S(2)}) copy-start(f32[2,32,128]{2,0,1:T(2,128)S(1)} %get-tuple-element.990) | copy-start | bytes 98308 | tf_op jit(solution)/shard_map/while
  210.0 4.6 %copy-start.16 = (f32[1,32,128]{2,0,1:T(1,128)}, f32[1,32,128]{2,0,1:T(1,128)S(1)}, u32[]{:S(2)}) copy-start(f32[1,32,128]{2,0,1:T(1,128)S(1)} %get-tuple-element.879) | copy-start | bytes 49156 | tf_op jit(solution)/shard_map/while
  210.0 4.5 %copy-start.10 = (f32[2,32,128]{2,0,1:T(2,128)}, f32[2,32,128]{2,0,1:T(2,128)S(1)}, u32[]{:S(2)}) copy-start(f32[2,32,128]{2,0,1:T(2,128)S(1)} %slice.255) | copy-start | bytes 98308 | tf_op jit(solution)/shard_map/while
  210.1 4.2 %copy-start.23 = (f32[4096]{0:T(1024)}, f32[4096]{0:T(1024)S(1)}, u32[]{:S(2)}) copy-start(f32[4096]{0:T(1024)S(1)} %bitcast_multiply_fusion.7) | copy-start | bytes 49156 | tf_op jit(solution)/shard_map/while
  214.5 5.6 %copy-start.51 = (f32[240]{0:T(256)S(1)}, f32[240]{0:T(256)}, u32[]{:S(2)}) copy-start(f32[240]{0:T(256)} %get-tuple-element.1000) | copy-start | bytes 2884 | tf_op jit(solution)/shard_map/while
  234.6 13.2 %copy-start.54 = (f32[2,3,32]{2,1,0:T(4,128)}, f32[2,3,32]{2,1,0:T(4,128)S(1)}, u32[]{:S(2)}) copy-start(f32[2,3,32]{2,1,0:T(4,128)S(1)} %get-tuple-element.989) | copy-start | bytes 2308 | tf_op jit(solution)/shard_map/while
  234.6 17.2 %copy-start.38 = (f32[2,32,128]{2,0,1:T(2,128)}, f32[2,32,128]{2,0,1:T(2,128)S(1)}, u32[]{:S(2)}) copy-start(f32[2,32,128]{2,0,1:T(2,128)S(1)} %get-tuple-element.986) | copy-start | bytes 98308 | tf_op jit(solution)/shard_map/while
  234.6 17.2 %copy-start.42 = (f32[2,32,128]{2,0,1:T(2,128)}, f32[2,32,128]{2,0,1:T(2,128)S(1)}, u32[]{:S(2)}) copy-start(f32[2,32,128]{2,0,1:T(2,128)S(1)} %get-tuple-element.990) | copy-start | bytes 98308 | tf_op jit(solution)/shard_map/while
  248.8 4.6 %copy-start.16 = (f32[1,32,128]{2,0,1:T(1,128)}, f32[1,32,128]{2,0,1:T(1,128)S(1)}, u32[]{:S(2)}) copy-start(f32[1,32,128]{2,0,1:T(1,128)S(1)} %get-tuple-element.879) | copy-start | bytes 49156 | tf_op jit(solution)/shard_map/while
  248.8 4.5 %copy-start.10 = (f32[2,32,128]{2,0,1:T(2,128)}, f32[2,32,128]{2,0,1:T(2,128)S(1)}, u32[]{:S(2)}) copy-start(f32[2,32,128]{2,0,1:T(2,128)S(1)} %slice.255) | copy-start | bytes 98308 | tf_op jit(solution)/shard_map/while
  248.9 4.2 %copy-start.23 = (f32[4096]{0:T(1024)}, f32[4096]{0:T(1024)S(1)}, u32[]{:S(2)}) copy-start(f32[4096]{0:T(1024)S(1)} %bitcast_multiply_fusion.7) | copy-start | bytes 49156 | tf_op jit(solution)/shard_map/while
  253.3 5.6 %copy-start.51 = (f32[240]{0:T(256)S(1)}, f32[240]{0:T(256)}, u32[]{:S(2)}) copy-start(f32[240]{0:T(256)} %get-tuple-element.1000) | copy-start | bytes 2884 | tf_op jit(solution)/shard_map/while
  276.9 71.4 %copy-start.46 = (f32[2,3,32,128]{3,1,2,0:T(4,128)S(1)}, f32[2,3,32,128]{3,1,2,0:T(4,128)}, u32[]{:S(2)}) copy-start(f32[2,3,32,128]{3,1,2,0:T(4,128)} %get-tuple-element.461) | copy-start | bytes 294916
  276.9 74.8 %copy-start.61 = (f32[3,64]{1,0:T(4,128)S(1)}, f32[3,64]{1,0:T(4,128)}, u32[]{:S(2)}) copy-start(f32[3,64]{1,0:T(4,128)} %get-tuple-element.614) | copy-start | bytes 2308
  347.7 2.2 collective-permute-start.7
  347.8 3.9 %collective-permute-start.6 = (f32[3,1,64]{2,0,1:T(4,128)S(1)}, f32[3,1,64]{2,0,1:T(4,128)S(1)}, u32[]{:S(2)}, u32[]{:S(2)}) collective-permute-start(f32[3,1,64]{2,0,1:T(4,128)S(1)} %copy.138), channel_id=1, source_target_pairs={{0,4},{4,8},{8,12},{12,16},{16,20},{20,24},{24,28},{28,0},{1,5},{5... | collective-permute-start | bytes 2312 | tf_op jit(solution)/shard_map/ppermute | solution.py:29
  (63 other events, 113.3 us)
Sparse Core Ops, SparseCore 0:
  148.2 24.1 reduce-scatter.6
  323.4 23.1 reduce-scatter.8
